TPU v7x, 32 devices: a whole 2x2x4 slice. The times are simulated.
32 devices in a mesh: outer: 8 (over z, core), inner: 4 (over y, x).
Axes of the slice: x: 2, y: 2, z: 4, core: 2. Of those that a mesh axis runs over, the one named last changes fastest.
Arguments:
- queries: bfloat16 [2048, 4096], P(('outer', 'inner')), may hold values from -6 to 6
- keys: bfloat16 [2048, 4096], P(('outer', 'inner')), may hold values from -6 to 6
- values: bfloat16 [2048, 4096], P(('outer', 'inner')), may hold values from -6 to 6
- lengths: int32 [16], replicated, may hold values from 1 to 32, 128 in all
- norm_gain: float32 [4096], replicated, may hold values from 0.5 to 1.5
Outputs:
- attended: bfloat16 [2048, 4096], P(('outer', 'inner'))
Inputs may be any that keep to these rules, and one draw needn't show every extreme that they name: The lengths sum to 128; one document is exactly 32 units long.
All inputs are finite; a program needn't handle non-finite values.
Results may differ from a plain program's by a relative error of at most 0.0049.
Values sent between devices are 32-bit elements; how exact they have to be, the bound alone decides.
No kernel may reach another device: no remote copies, remote signals or barrier semaphores. Data moves between devices by JAX's collectives and lax.ppermute only.
A program may use at most 64 MiB of HBM per device.

v0:
```python
import jax
import jax.numpy as jnp
from jax import lax
from jax.sharding import PartitionSpec as P

HEAD_DIM = 128
BLOCK = 16
EPSILON = 1e-05


def carried_in(shard, axis, combine, identity):
    devices, index = (lax.axis_size(axis), lax.axis_index(axis))
    everything = jax.tree.map(lambda part: lax.all_gather(part, axis), shard)
    start = jax.tree.map(
        lambda part, zero: jnp.broadcast_to(jnp.asarray(zero, part.dtype), part.shape),
        shard,
        identity,
    )

    def lap(k, before):
        reached = k < index
        new = combine(before, jax.tree.map(lambda part: part[k], everything))
        return jax.tree.map(lambda a, b: jnp.where(reached, a, b), new, before)

    return lax.fori_loop(0, devices, lap, start)


def join_states(earlier, later):
    return (jnp.maximum(earlier[0], later[0]), later[1] + (1.0 - later[0]) * earlier[1])


def doc_ids(tok_rows, doc_starts):
    return jnp.sum((tok_rows[:, None] >= doc_starts[None, :]).astype(jnp.int32), axis=1) - 1


def body(queries, keys, values, lengths, norm_gain):
    tok_count = queries.shape[0]
    head_count = queries.shape[1] // HEAD_DIM
    state_rows = head_count * HEAD_DIM
    inner_count = lax.axis_size("inner")
    share_rows = state_rows // inner_count
    inner_place = lax.axis_index("inner")
    outer_place = lax.axis_index("outer")
    device_place = outer_place * inner_count + inner_place
    first_row = device_place * tok_count
    tok_rows = first_row + jnp.arange(tok_count, dtype=jnp.int32)
    doc_starts = BLOCK * (jnp.cumsum(lengths) - lengths)
    docs = doc_ids(tok_rows, doc_starts)
    first_doc = docs[0]
    final_doc = docs[-1]
    opens_block = jnp.any(doc_starts == first_row).astype(jnp.float32)
    group_places = outer_place * inner_count + jnp.arange(inner_count, dtype=jnp.int32)
    group_first = group_places * tok_count
    block_flags = jnp.any(
        (doc_starts[None, :] >= group_first[:, None])
        & (doc_starts[None, :] < group_first[:, None] + tok_count),
        axis=1,
    ).astype(jnp.float32)
    query_heads = queries.reshape(tok_count, head_count, HEAD_DIM)
    key_heads = keys.reshape(tok_count, head_count, HEAD_DIM)
    value_heads = values.reshape(tok_count, head_count, HEAD_DIM)
    final_keys = jnp.where((docs == final_doc)[:, None, None], key_heads, jnp.zeros_like(key_heads))
    local_state = jnp.einsum(
        "thd,the->hde", final_keys, value_heads, preferred_element_type=jnp.float32
    )
    shares = lax.all_to_all(
        local_state.reshape(1, state_rows, HEAD_DIM),
        "inner",
        split_axis=1,
        concat_axis=0,
        tiled=True,
    )
    scores = jnp.einsum("thd,shd->hts", query_heads, key_heads, preferred_element_type=jnp.float32)
    allowed = (tok_rows[:, None] >= tok_rows[None, :]) & (docs[:, None] == docs[None, :])
    weights = jnp.where(allowed[None], scores, 0.0).astype(jnp.bfloat16)
    intra = jnp.einsum("hts,she->the", weights, value_heads, preferred_element_type=jnp.float32)

    def walk(carried, item):
        return (join_states(carried, item), carried)

    share_zero = (jnp.float32(0.0), jnp.zeros((share_rows, HEAD_DIM), jnp.float32))
    group_total, earlier_in_group = lax.scan(walk, share_zero, (block_flags, shares))
    outer_prefix = carried_in(group_total, "outer", join_states, share_zero)
    combined = (
        earlier_in_group[1] + (1.0 - earlier_in_group[0])[:, None, None] * outer_prefix[1][None]
    )
    returned = lax.all_to_all(combined, "inner", split_axis=0, concat_axis=1, tiled=True)
    prefix_state = returned.reshape(head_count, HEAD_DIM, HEAD_DIM)
    carry_in = (1.0 - opens_block) * prefix_state
    held = carry_in.astype(jnp.bfloat16)
    inter = jnp.einsum("thd,hde->the", query_heads, held, preferred_element_type=jnp.float32)
    inter = jnp.where((docs == first_doc)[:, None, None], inter, 0.0)
    mixed = intra + inter
    scale = lax.rsqrt(jnp.mean(mixed * mixed, axis=-1, keepdims=True) + EPSILON)
    gain_heads = norm_gain.reshape(head_count, HEAD_DIM)
    attended = (mixed * scale * gain_heads[None]).astype(jnp.bfloat16)
    return attended.reshape(tok_count, head_count * HEAD_DIM)


def solution(mesh):
    placed = (
        P(("outer", "inner"), None),
        P(("outer", "inner"), None),
        P(("outer", "inner"), None),
        P(),
        P(),
    )
    return jax.shard_map(
        body, mesh=mesh, in_specs=placed, out_specs=P(("outer", "inner"), None), check_vma=False
    )
```

profile of v0, /device:TPU:0, one launch (start us, length us, event | category | flops | bytes accessed | tf_op | source)
XLA Modules:
  0.0 167.0 jit_solution(1256728201418256629)
XLA Ops:
  6.5 0.0 copy-start
  6.5 0.8 copy.26
  7.4 0.1 reduce
  7.5 1.4 compare_reduce_fusion
  8.9 0.1 convert_reduce_fusion
  9.0 0.6 fusion.27
  9.6 1.3 broadcast_compare_fusion.1
  10.9 0.0 copy-done
  10.9 2.9 %fusion.5 = f32[32,128,128]{2,1,0:T(8,128)} fusion(pred[64]{0:T(512)(128)(4,1)S(1)} %get-tuple-element.213, bf16[64,4096]{1,0:T(8,128)(2,1)S(1)} %copy-done, bf16[64,4096]{1,0:T(8,128)(2,1)} %param.10), kind=kOutput, calls=%fused_computation.16 | convolution fusion | flops 67371008 | bytes 3145792 | tf_op jit(solution)/shard_map/thd,the->hde/dot_general | solution.py:63
  13.8 5.2 %all-to-all-start = ((f32[1,4096,128]{2,0,1:T(1,128)}), f32[1,4096,128]{2,0,1:T(1,128)S(1)}, u32[]{:S(2)}, u32[]{:S(2)}) async-start(f32[1,4096,128]{2,0,1:T(1,128)} %bitcast.90), calls=%async_computation | async-start | bytes 4194304 | tf_op jit(solution)/shard_map/all_to_all | solution.py:66
  19.0 0.2 and_reduce_fusion
  19.2 24.6 %all-to-all-done = f32[1,4096,128]{2,0,1:T(1,128)S(1)} async-done(((f32[1,4096,128]{2,0,1:T(1,128)}), f32[1,4096,128]{2,0,1:T(1,128)S(1)}, u32[]{:S(2)}, u32[]{:S(2)}) %all-to-all-start) | async-done | bytes 2097184 | tf_op jit(solution)/shard_map/all_to_all | solution.py:66
  43.8 12.1 %while.31 = (s32[]{:T(128)}, f32[]{:T(128)}, f32[1024,128]{1,0:T(8,128)S(1)}, f32[4]{0:T(128)S(1)}, f32[4,1024,128]{2,1,0:T(8,128)}, /*index=5*/f32[4]{0:T(128)S...) while((s32[]{:T(128)}, f32[]{:T(128)}, f32[1024,128]{1,0:T(8,128)S(1)}, ...), condition=%wide.region_5.6_spmd.clone, body=%wide.region_4.5_spmd.clone.sunk | while | flops 524293 | bytes 2622128 | solution.py:82
  43.8 0.8 bitcast_dynamic-update-slice_fusion.2
  44.7 0.6 dynamic_slice.33
  46.0 0.1 bitcast_add_fusion.3
  46.7 0.1 dynamic_update_slice.14
  46.8 0.8 bitcast_dynamic-update-slice_fusion.2
  47.7 0.6 dynamic_slice.33
  49.0 0.1 bitcast_add_fusion.3
  49.8 0.1 dynamic_update_slice.14
  49.9 0.8 bitcast_dynamic-update-slice_fusion.2
  50.7 0.6 dynamic_slice.33
  52.0 0.1 bitcast_add_fusion.3
  52.8 0.1 dynamic_update_slice.14
  52.9 0.8 bitcast_dynamic-update-slice_fusion.2
  53.7 0.6 dynamic_slice.33
  55.0 0.1 bitcast_add_fusion.3
  55.8 0.1 dynamic_update_slice.14
  55.9 0.8 copy-done.1
  56.7 0.0 all-gather.3.cloned.1.call-update
  56.8 0.7 dynamic-slice
  57.4 0.8 dynamic-update-slice
  58.2 16.4 %all-reduce = f32[8]{0:T(128)S(1)} all-reduce(f32[8]{0:T(128)S(1)} %dynamic-update-slice), channel_id=1, replica_groups=mesh['outer'=8,'inner'=4] {'outer'}, use_global_device_ids=true, to_apply=%add | all-reduce | flops 8 | bytes 64
  74.6 29.9 %all-gather.3.cloned.1.call-done = f32[8192,128]{1,0:T(8,128)} async-done(((f32[1024,128]{1,0:T(8,128)}), f32[8192,128]{1,0:T(8,128)}) %all-gather.3.cloned.1.call-update) | async-done | bytes 4194320 | tf_op jit(solution)/shard_map/all_gather | solution.py:13
  104.5 21.9 %while.32 = (s32[]{:T(128)}, f32[1024,128]{1,0:T(8,128)S(1)}, s32[]{:T(128)}, f32[8,1024,128]{2,1,0:T(8,128)}, f32[8]{0:T(128)S(1)}, /*index=5*/s32[]{:T(128)}, f32[1]{0:T(128)}, s32[]{:T(128)}) while((s32[]{:T(128)}, f32[1024,128]{1,0:T(8,128)S(1)}, s32[]{:T(128)}, f32[8,1024,128]{2,1,0:T(8,128)}, f32[8]{0:T(128)S(1)}, ...), condition=%wide.region_7.8_spmd.clone, body=%wide.region_6.7_spmd.clone.sunk | while | flops 524293 | bytes 1573001 | solution.py:25
  104.5 0.6 dynamic_slice.35
  105.8 1.5 fusion.37
  107.3 0.6 dynamic_slice.35
  108.5 1.5 fusion.37
  110.0 0.6 dynamic_slice.35
  111.2 1.5 fusion.37
  112.7 0.6 dynamic_slice.35
  114.0 1.5 fusion.37
  115.5 0.6 dynamic_slice.35
  116.7 1.5 fusion.37
  118.2 0.6 dynamic_slice.35
  119.5 1.5 fusion.37
  120.9 0.6 dynamic_slice.35
  122.2 1.5 fusion.37
  123.7 0.6 dynamic_slice.35
  124.9 1.5 fusion.37
  126.4 0.0 copy-done.2
  126.4 1.6 multiply_add_fusion
  128.0 4.0 %all-to-all-start.1 = ((f32[4,1024,128]{2,1,0:T(8,128)}), f32[4,1024,128]{2,1,0:T(8,128)S(1)}, u32[]{:S(2)}, u32[]{:S(2)}) async-start(f32[4,1024,128]{2,1,0:T(8,128)} %multiply_add_fusion), calls=%async_computation.1 | async-start | bytes 4194304 | tf_op jit(solution)/shard_map/all_to_all | solution.py:87
  132.6 0.1 compare_and_fusion
  132.7 0.0 copy-done.4
  132.7 2.6 %convolution_bitcast_fusion = f32[64,32,128]{2,0,1:T(8,128)} fusion(pred[64,64]{1,0:T(8,128)(4,1)S(1)} %compare_and_fusion, bf16[64,4096]{1,0:T(8,128)(2,1)S(1)} %copy-done, bf16[64,4096]{1,0:T(8,128)(2,1)S(1)} %copy-done.4, bf16[64,4096]{1,0:T(8,128)(2,1)} %param.9), kind=kOutput, calls=%fused_computation.10 | convolution fusion | flops 67371008 | bytes 2625536 | tf_op jit(solution)/shard_map/hts,she->the/dot_general | solution.py:76
  135.3 22.0 %all-to-all-done.1 = f32[4,1024,128]{2,1,0:T(8,128)S(1)} async-done(((f32[4,1024,128]{2,1,0:T(8,128)}), f32[4,1024,128]{2,1,0:T(8,128)S(1)}, u32[]{:S(2)}, u32[]{:S(2)}) %all-to-all-start.1) | async-done | bytes 2097184 | tf_op jit(solution)/shard_map/all_to_all | solution.py:87
  157.3 0.2 multiply_convert_fusion
  157.4 0.0 copy-start.6
  157.5 1.0 copy-done.3
  158.5 0.5 multiply_reduce_fusion
  159.0 1.1 copy_bitcast_fusion
  (22 shorter events, 0.1 us)
Async XLA Ops:
  6.5 4.3 %copy-start = (bf16[64,4096]{1,0:T(8,128)(2,1)S(1)}, bf16[64,4096]{1,0:T(8,128)(2,1)}, u32[]{:S(2)}) copy-start(bf16[64,4096]{1,0:T(8,128)(2,1)} %param.11) | copy-start | bytes 1572868
  13.8 30.0 %all-to-all-start = ((f32[1,4096,128]{2,0,1:T(1,128)}), f32[1,4096,128]{2,0,1:T(1,128)S(1)}, u32[]{:S(2)}, u32[]{:S(2)}) async-start(f32[1,4096,128]{2,0,1:T(1,128)} %bitcast.90), calls=%async_computation | async-start | bytes 4194304 | tf_op jit(solution)/shard_map/all_to_all | solution.py:66
  19.0 85.6 %all-gather.3.cloned.1.call-start = ((), (), s32[]{:S(2)}) async-start(), calls=%async_computation.2 | async-start | bytes 4718592 | tf_op jit(solution)/shard_map/all_gather | solution.py:13
  43.8 12.9 %copy-start.7 = (u32[32]{0:T(128)S(1)}, u32[32]{0:T(128)}, u32[]{:S(2)}) copy-start(u32[32]{0:T(128)} %constant.84) | copy-start | bytes 388
  55.9 0.8 copy-start.1
  55.9 70.5 %copy-start.2 = (f32[4,1024,128]{2,1,0:T(8,128)S(1)}, f32[4,1024,128]{2,1,0:T(8,128)}, u32[]{:S(2)}) copy-start(f32[4,1024,128]{2,1,0:T(8,128)} %get-tuple-element.139) | copy-start | bytes 6291460
  128.0 4.7 %copy-start.4 = (bf16[64,4096]{1,0:T(8,128)(2,1)S(1)}, bf16[64,4096]{1,0:T(8,128)(2,1)}, u32[]{:S(2)}) copy-start(bf16[64,4096]{1,0:T(8,128)(2,1)} %param.10) | copy-start | bytes 1572868
  128.0 29.3 %all-to-all-start.1 = ((f32[4,1024,128]{2,1,0:T(8,128)}), f32[4,1024,128]{2,1,0:T(8,128)S(1)}, u32[]{:S(2)}, u32[]{:S(2)}) async-start(f32[4,1024,128]{2,1,0:T(8,128)} %multiply_add_fusion), calls=%async_computation.1 | async-start | bytes 4194304 | tf_op jit(solution)/shard_map/all_to_all | solution.py:87
  135.3 22.2 %copy-start.5 = (bf16[64,4096]{1,0:T(8,128)(2,1)S(1)}, bf16[64,4096]{1,0:T(8,128)(2,1)}, u32[]{:S(2)}) copy-start(bf16[64,4096]{1,0:T(8,128)(2,1)} %param.9) | copy-start | bytes 1572868
  157.3 1.2 copy-start.3
  157.4 1.6 copy-start.6
Sparse Core Ops, SparseCore 0:
  56.8 47.6 all-gather.2
where the time goes:
time: 168 us; the launch traced here: 167 us
  waiting for transfers between devices  76.5 us (46%)
  other arithmetic  21.8 us (13%)
  blocking collectives  16.4 us (10%)
  between operations  14.2 us (8%)
  local copies, waits for them, and re-layouts  12.4 us (7%)
  loops' own time  10.5 us (6%)
  starting transfers between devices  9.12 us (5%)
  matrix products  6.03 us (4%)
    all_gather x1, waiting for transfers between devices, carried_in(): everything = jax.tree.map(lambda part: lax.all_gather(part, axis), shard)  29.9 us
    all_to_all x1, waiting for transfers between devices, body(): lax.all_to_all(local_state.reshape(1, state_rows, HEAD_DIM), 'inner', spl...  24.6 us
    all_to_all x1, waiting for transfers between devices, body(): lax.all_to_all(combined, 'inner', split_axis=0, concat_axis=1, tiled=True)  22 us
    unnamed x1, blocking collectives  16.4 us
    select_n x8, other arithmetic, lap(): return jax.tree.map(lambda a, b: jnp.where(reached, a, b), new, before)  11.8 us
    another operation x1, loops' own time, carried_in(): return lax.fori_loop(0, devices, lap, start)  5.38 us
    all_to_all x1, starting transfers between devices, body(): lax.all_to_all(local_state.reshape(1, state_rows, HEAD_DIM), 'inner', spl...  5.17 us
    another operation x1, loops' own time, body(): lax.scan(walk, share_zero, (block_flags, shares))  5.11 us
  transfers between devices with their start and end apart: 3, of which 3 were waited for; matrix products, arithmetic and copies ran while one was open for 3% of the time, Pallas kernels for 0%

commit v1 on v0

--- a/solution.py
+++ b/solution.py
@@ -6,6 +6,29 @@
 HEAD_DIM = 128
 BLOCK = 16
 EPSILON = 1e-05
+
+
+def in_blocks(x, dim, size):
+    shape = x.shape
+    pieces = x.reshape(*shape[:dim], size, shape[dim] // size, *shape[dim + 1 :])
+    return jnp.moveaxis(pieces, dim, 0)
+
+
+def joined_along(blocks, dim):
+    blocks = jnp.moveaxis(blocks, 0, dim)
+    shape = blocks.shape
+    return blocks.reshape(*shape[:dim], shape[dim] * shape[dim + 1], *shape[dim + 2 :])
+
+
+def pairwise_exchange(x, axis, split_dim, concat_dim):
+    size, index = (lax.axis_size(axis), lax.axis_index(axis))
+    blocks = in_blocks(x, split_dim, size)
+    done = [blocks[index]]
+    for turn in range(1, size):
+        sent = blocks[index ^ turn]
+        done.append(lax.ppermute(sent, axis, [(i, i ^ turn) for i in range(size)]))
+    blocks = jnp.stack(done)[index ^ jnp.arange(size)]
+    return joined_along(blocks, concat_dim)
 
 
 def carried_in(shard, axis, combine, identity):
@@ -84,7 +107,7 @@
     combined = (
         earlier_in_group[1] + (1.0 - earlier_in_group[0])[:, None, None] * outer_prefix[1][None]
     )
-    returned = lax.all_to_all(combined, "inner", split_axis=0, concat_axis=1, tiled=True)
+    returned = pairwise_exchange(combined, "inner", 0, 1)
     prefix_state = returned.reshape(head_count, HEAD_DIM, HEAD_DIM)
     carry_in = (1.0 - opens_block) * prefix_state
     held = carry_in.astype(jnp.bfloat16)

time: 168 us -> 168 us (level)
  other arithmetic: 21.8 us -> 23.7 us
  local copies, waits for them, and re-layouts: 12.4 us -> 14.1 us
    all_to_all x1 -> x0, waiting for transfers between devices: 22 us -> none  [body(): lax.all_to_all(combined, 'inner', split_axis=0, concat_axis=1, tiled=True)]
    ppermute x0 -> x3, waiting for transfers between devices: none -> 20.7 us  [pairwise_exchange(): done.append(lax.ppermute(sent, axis, [(i, i ^ turn) for i in range(size)]))]
    all_to_all x1 -> x0, starting transfers between devices: 3.96 us -> none  [body(): lax.all_to_all(combined, 'inner', split_axis=0, concat_axis=1, tiled=True)]
    ppermute x0 -> x3, starting transfers between devices: none -> 3.49 us  [pairwise_exchange(): done.append(lax.ppermute(sent, axis, [(i, i ^ turn) for i in range(size)]))]
    gather x0 -> x1, local copies, waits for them, and re-layouts: none -> 2.01 us  [pairwise_exchange(): blocks = jnp.stack(done)[index ^ jnp.arange(size)]]
    convert_element_type x1, other arithmetic: 0.17 us -> 1.87 us  [body(): held = carry_in.astype(jnp.bfloat16)]
  transfers between devices with their start and end apart: 3 -> 5, of which waited for: 3 -> 5; matrix products, arithmetic and copies ran while one was open for 3% -> 2% of each run, Pallas kernels for 0% -> 0%
where the time goes in v1:
time: 168 us; the launch traced here: 167 us
  waiting for transfers between devices  75.4 us (45%)
  other arithmetic  23.7 us (14%)
  blocking collectives  16.4 us (10%)
  between operations  14.3 us (9%)
  local copies, waits for them, and re-layouts  14.1 us (8%)
  loops' own time  9.91 us (6%)
  starting transfers between devices  8.66 us (5%)
  matrix products  4.97 us (3%)
    all_gather x1, waiting for transfers between devices, carried_in(): everything = jax.tree.map(lambda part: lax.all_gather(part, axis), shard)  30 us
    all_to_all x1, waiting for transfers between devices, body(): lax.all_to_all(local_state.reshape(1, state_rows, HEAD_DIM), 'inner', spl...  24.6 us
    ppermute x3, waiting for transfers between devices, pairwise_exchange(): done.append(lax.ppermute(sent, axis, [(i, i ^ turn) for i in range(size)]))  20.7 us
    unnamed x1, blocking collectives  16.4 us
    select_n x8, other arithmetic, lap(): return jax.tree.map(lambda a, b: jnp.where(reached, a, b), new, before)  11.8 us
    another operation x1, loops' own time, carried_in(): return lax.fori_loop(0, devices, lap, start)  5.38 us
    all_to_all x1, starting transfers between devices, body(): lax.all_to_all(local_state.reshape(1, state_rows, HEAD_DIM), 'inner', spl...  5.17 us
    dynamic_slice x8, local copies, waits for them, and re-layouts, lap(): new = combine(before, jax.tree.map(lambda part: part[k], everything))  4.69 us
  transfers between devices with their start and end apart: 5, of which 5 were waited for; matrix products, arithmetic and copies ran while one was open for 2% of the time, Pallas kernels for 0%

profile of v1, /device:TPU:0, one launch (start us, length us, event | category | flops | bytes accessed | tf_op | source)
XLA Modules:
  0.0 167.4 jit_solution(3239970305296384705)
XLA Ops:
  6.5 0.8 copy.26
  7.4 0.1 reduce
  7.5 1.4 compare_reduce_fusion
  8.9 0.1 convert_reduce_fusion
  9.0 0.6 fusion.28
  9.6 1.3 broadcast_compare_fusion.1
  10.8 2.9 %fusion.5 = f32[32,128,128]{2,1,0:T(8,128)} fusion(pred[64]{0:T(512)(128)(4,1)S(1)} %get-tuple-element.217, bf16[64,4096]{1,0:T(8,128)(2,1)S(1)} %copy-done, bf16[64,4096]{1,0:T(8,128)(2,1)} %param.10), kind=kOutput, calls=%fused_computation.18 | convolution fusion | flops 67371008 | bytes 3145792 | tf_op jit(solution)/shard_map/thd,the->hde/dot_general | solution.py:86
  13.8 5.2 %all-to-all-start = ((f32[1,4096,128]{2,0,1:T(1,128)}), f32[1,4096,128]{2,0,1:T(1,128)S(1)}, u32[]{:S(2)}, u32[]{:S(2)}) async-start(f32[1,4096,128]{2,0,1:T(1,128)} %bitcast.99), calls=%async_computation | async-start | bytes 4194304 | tf_op jit(solution)/shard_map/all_to_all | solution.py:89
  19.0 0.2 and_reduce_fusion
  19.2 24.6 %all-to-all-done = f32[1,4096,128]{2,0,1:T(1,128)S(1)} async-done(((f32[1,4096,128]{2,0,1:T(1,128)}), f32[1,4096,128]{2,0,1:T(1,128)S(1)}, u32[]{:S(2)}, u32[]{:S(2)}) %all-to-all-start) | async-done | bytes 2097184 | tf_op jit(solution)/shard_map/all_to_all | solution.py:89
  43.8 11.2 %while.31 = (s32[]{:T(128)}, f32[]{:T(128)}, f32[1024,128]{1,0:T(8,128)S(1)}, f32[4]{0:T(128)S(1)}, f32[4,1024,128]{2,1,0:T(8,128)}, /*index=5*/f32[4]{0:T(128)S...) while((s32[]{:T(128)}, f32[]{:T(128)}, f32[1024,128]{1,0:T(8,128)S(1)}, ...), condition=%wide.region_5.6_spmd.clone, body=%wide.region_4.5_spmd.clone.sunk | while | flops 524293 | bytes 2622128 | solution.py:105
  43.8 0.9 bitcast_dynamic-update-slice_fusion.2
  44.7 0.6 dynamic_slice.40
  45.8 0.1 bitcast_add_fusion.3
  46.5 0.1 dynamic_update_slice.14
  46.6 0.8 bitcast_dynamic-update-slice_fusion.2
  47.5 0.6 dynamic_slice.40
  48.6 0.1 bitcast_add_fusion.3
  49.3 0.1 dynamic_update_slice.14
  49.4 0.8 bitcast_dynamic-update-slice_fusion.2
  50.3 0.6 dynamic_slice.40
  51.4 0.1 bitcast_add_fusion.3
  52.1 0.1 dynamic_update_slice.14
  52.2 0.8 bitcast_dynamic-update-slice_fusion.2
  53.1 0.6 dynamic_slice.40
  54.2 0.1 bitcast_add_fusion.3
  54.9 0.1 dynamic_update_slice.14
  55.0 0.8 copy-done.1
  55.9 0.6 dynamic-slice.7
  56.5 0.7 dynamic-update-slice
  57.2 16.4 %all-reduce = f32[8]{0:T(128)S(1)} all-reduce(f32[8]{0:T(128)S(1)} %dynamic-update-slice), channel_id=1, replica_groups=mesh['outer'=8,'inner'=4] {'outer'}, use_global_device_ids=true, to_apply=%add | all-reduce | flops 8 | bytes 64
  73.7 30.0 %all-gather.3.cloned.1.call-done = f32[8192,128]{1,0:T(8,128)} async-done(((f32[1024,128]{1,0:T(8,128)}), f32[8192,128]{1,0:T(8,128)}) %all-gather.3.cloned.1.call-update) | async-done | bytes 4194320 | tf_op jit(solution)/shard_map/all_gather | solution.py:36
  103.7 21.9 %while.32 = (s32[]{:T(128)}, f32[1024,128]{1,0:T(8,128)S(1)}, s32[]{:T(128)}, f32[8,1024,128]{2,1,0:T(8,128)}, f32[8]{0:T(128)S(1)}, /*index=5*/s32[]{:T(128)}, f32[1]{0:T(128)}, s32[]{:T(128)}) while((s32[]{:T(128)}, f32[1024,128]{1,0:T(8,128)S(1)}, s32[]{:T(128)}, f32[8,1024,128]{2,1,0:T(8,128)}, f32[8]{0:T(128)S(1)}, ...), condition=%wide.region_7.8_spmd.clone, body=%wide.region_6.7_spmd.clone.sunk | while | flops 524293 | bytes 1573001 | solution.py:48
  103.7 0.6 dynamic_slice.42
  104.9 1.5 fusion.38
  106.4 0.6 dynamic_slice.42
  107.6 1.5 fusion.38
  109.1 0.6 dynamic_slice.42
  110.4 1.5 fusion.38
  111.9 0.6 dynamic_slice.42
  113.1 1.5 fusion.38
  114.6 0.6 dynamic_slice.42
  115.8 1.5 fusion.38
  117.3 0.6 dynamic_slice.42
  118.6 1.5 fusion.38
  120.1 0.6 dynamic_slice.42
  121.3 1.5 fusion.38
  122.8 0.6 dynamic_slice.42
  124.0 1.5 fusion.38
  125.5 0.2 multiply_add_fusion
  125.8 0.9 dynamic-slice_bitcast_fusion
  126.8 1.4 collective-permute-start
  128.2 1.7 %collective-permute-start.1 = (f32[1,1024,128]{2,1,0:T(8,128)S(1)}, f32[1,1024,128]{2,1,0:T(8,128)}, u32[]{:S(2)}, u32[]{:S(2)}) collective-permute-start(f32[1,1024,128]{2,1,0:T(8,128)S(1)} %get-tuple-element.214), channel_id=1, source_target_pairs={{0,2},{1,3},{2,0},{3,1},{4,6},{5,7},{6,4},{7,5},{8,10},{9,11},{10,... | collective-permute-start | bytes 1572872 | tf_op jit(solution)/shard_map/ppermute | solution.py:29
  129.9 0.3 collective-permute-start.2
  131.1 1.6 convolution_bitcast_fusion
  132.6 9.2 %collective-permute-done = f32[1,1024,128]{2,1,0:T(8,128)} collective-permute-done((f32[1,1024,128]{2,1,0:T(8,128)}, f32[1,1024,128]{2,1,0:T(8,128)}, u32[]{:S(2)}, u32[]{:S(2)}) %collective-permute-start) | collective-permute-done | bytes 524320 | tf_op jit(solution)/shard_map/ppermute | solution.py:29
  141.8 10.6 %collective-permute-done.1 = f32[1,1024,128]{2,1,0:T(8,128)} collective-permute-done((f32[1,1024,128]{2,1,0:T(8,128)S(1)}, f32[1,1024,128]{2,1,0:T(8,128)}, u32[]{:S(2)}, u32[]{:S(2)}) %collective-permute-start.1) | collective-permute-done | bytes 524320 | tf_op jit(solution)/shard_map/ppermute | solution.py:29
  152.5 0.8 collective-permute-done.2
  153.3 1.5 maximum_bitcast_fusion
  154.8 2.0 %gather_fusion = f32[4,1024,128]{2,1,0:T(8,128)} fusion(f32[4,1024,128]{2,1,0:T(8,128)S(1)} %maximum_bitcast_fusion, s32[1024]{0:T(1024)S(1)} %pad_clamp_fusion), kind=kCustom, calls=%fused_computation | custom fusion | bytes 4194320 | tf_op jit(solution)/shard_map/gather | solution.py:30
  156.8 1.9 %multiply_convert_fusion = bf16[4,1024,128]{2,1,0:T(8,128)(2,1)S(1)} fusion(f32[4,1024,128]{2,1,0:T(8,128)} %gather_fusion, f32[]{:T(128)S(6)} %sub.28), kind=kLoop, calls=%fused_computation.6 | loop fusion | flops 1048576 | bytes 3145732 | tf_op jit(solution)/shard_map/convert_element_type | solution.py:113
  158.8 0.5 multiply_reduce_fusion
  159.3 0.1 copy-done.7
  159.4 1.1 copy_bitcast_fusion
  (33 shorter events, 0.3 us)
Async XLA Ops:
  6.5 4.3 %copy-start = (bf16[64,4096]{1,0:T(8,128)(2,1)S(1)}, bf16[64,4096]{1,0:T(8,128)(2,1)}, u32[]{:S(2)}) copy-start(bf16[64,4096]{1,0:T(8,128)(2,1)} %param.11) | copy-start | bytes 1572868
  13.8 30.0 %all-to-all-start = ((f32[1,4096,128]{2,0,1:T(1,128)}), f32[1,4096,128]{2,0,1:T(1,128)S(1)}, u32[]{:S(2)}, u32[]{:S(2)}) async-start(f32[1,4096,128]{2,0,1:T(1,128)} %bitcast.99), calls=%async_computation | async-start | bytes 4194304 | tf_op jit(solution)/shard_map/all_to_all | solution.py:89
  18.9 84.7 %all-gather.3.cloned.1.call-start = ((), (), s32[]{:S(2)}) async-start(), calls=%async_computation.1 | async-start | bytes 4718592 | tf_op jit(solution)/shard_map/all_gather | solution.py:36
  43.8 12.1 %copy-start.8 = (u32[32]{0:T(128)S(1)}, u32[32]{0:T(128)}, u32[]{:S(2)}) copy-start(u32[32]{0:T(128)} %constant.92) | copy-start | bytes 388
  55.0 0.8 copy-start.1
  55.0 70.5 %copy-start.2 = (f32[4,1024,128]{2,1,0:T(8,128)S(1)}, f32[4,1024,128]{2,1,0:T(8,128)}, u32[]{:S(2)}) copy-start(f32[4,1024,128]{2,1,0:T(8,128)} %get-tuple-element.139) | copy-start | bytes 6291460
  125.8 5.3 %copy-start.4 = (bf16[64,4096]{1,0:T(8,128)(2,1)S(1)}, bf16[64,4096]{1,0:T(8,128)(2,1)}, u32[]{:S(2)}) copy-start(bf16[64,4096]{1,0:T(8,128)(2,1)} %param.10) | copy-start | bytes 1572868
  125.8 5.2 %copy-start.5 = (bf16[64,4096]{1,0:T(8,128)(2,1)S(1)}, bf16[64,4096]{1,0:T(8,128)(2,1)}, u32[]{:S(2)}) copy-start(bf16[64,4096]{1,0:T(8,128)(2,1)} %param.9) | copy-start | bytes 1572868
  126.8 15.1 %collective-permute-start = (f32[1,1024,128]{2,1,0:T(8,128)}, f32[1,1024,128]{2,1,0:T(8,128)}, u32[]{:S(2)}, u32[]{:S(2)}) collective-permute-start(f32[1,1024,128]{2,1,0:T(8,128)} %get-tuple-element.215), channel_id=1, source_target_pairs={{0,1},{1,0},{2,3},{3,2},{4,5},{5,4},{6,7},{7,6},{8,9},{9,8},{10,11... | collective-permute-start | bytes 1572872 | tf_op jit(solution)/shard_map/ppermute | solution.py:29
  128.2 24.3 %collective-permute-start.1 = (f32[1,1024,128]{2,1,0:T(8,128)S(1)}, f32[1,1024,128]{2,1,0:T(8,128)}, u32[]{:S(2)}, u32[]{:S(2)}) collective-permute-start(f32[1,1024,128]{2,1,0:T(8,128)S(1)} %get-tuple-element.214), channel_id=1, source_target_pairs={{0,2},{1,3},{2,0},{3,1},{4,6},{5,7},{6,4},{7,5},{8,10},{9,11},{10,... | collective-permute-start | bytes 1572872 | tf_op jit(solution)/shard_map/ppermute | solution.py:29
  129.9 23.4 %collective-permute-start.2 = (f32[1,1024,128]{2,1,0:T(8,128)S(1)}, f32[1,1024,128]{2,1,0:T(8,128)}, u32[]{:S(2)}, u32[]{:S(2)}) collective-permute-start(f32[1,1024,128]{2,1,0:T(8,128)S(1)} %get-tuple-element.213), channel_id=1, source_target_pairs={{0,3},{1,2},{2,1},{3,0},{4,7},{5,6},{6,5},{7,4},{8,11},{9,10},{10,... | collective-permute-start | bytes 1572872 | tf_op jit(solution)/shard_map/ppermute | solution.py:29
  156.8 1.9 %copy-start.3 = (f32[64,32,128]{2,0,1:T(8,128)S(1)}, f32[64,32,128]{2,0,1:T(8,128)}, u32[]{:S(2)}) copy-start(f32[64,32,128]{2,0,1:T(8,128)} %convolution_bitcast_fusion) | copy-start | bytes 3145732
  156.8 2.0 %copy-start.6 = (bf16[64,4096]{1,0:T(8,128)(2,1)S(1)}, bf16[64,4096]{1,0:T(8,128)(2,1)}, u32[]{:S(2)}) copy-start(bf16[64,4096]{1,0:T(8,128)(2,1)} %param.9) | copy-start | bytes 1572868
  158.7 0.7 copy-start.7
Sparse Core Ops, SparseCore 0:
  56.0 47.6 all-gather.2
